TPU v7x, 32 devices: a whole 2x2x4 slice. The times are simulated.
32 devices in a mesh: row: 4 (over y, x), col: 8 (over z, core).
Axes of the slice: x: 2, y: 2, z: 4, core: 2. Of those that a mesh axis runs over, the one named last changes fastest.
Arguments:
- pair_rep: float32 [64, 64, 128], P('row', 'col'), may hold values from -160 to 160
- ln_gain: float32 [128], replicated, may hold values from 0.25 to 1.75
- ln_bias: float32 [128], replicated, may hold values from -3 to 3
- w_in: float32 [1024, 128], replicated, may hold values from -0.5 to 0.5
- w_out: float32 [512, 128], replicated, may hold values from -0.25 to 0.25
- w_pde: float32 [128, 64], replicated, may hold values from -2 to 2
- labels: int32 [64, 64], P('row', 'col'), may hold values from 0 to 63
- pair_mask: int32 [64, 64], P('row', 'col'), may hold values from 0 to 1, as said below
Outputs:
- mean_loss: float32 [], replicated
- d_pair_rep: float32 [64, 64, 128], P('row', 'col')
- d_ln_gain: float32 [128], replicated
- d_ln_bias: float32 [128], replicated
- d_w_in: float32 [1024, 128], P(('row', 'col'))
- d_w_out: float32 [512, 128], P(('row', 'col'))
- d_w_pde: float32 [128, 64], replicated
Inputs may be any that keep to these rules, and one draw needn't show every extreme that they name: pair_mask[i][j] = m_i m_j for a flag m_i of token i, with m_i = 1 whenever i is a multiple of 16.
All inputs are finite; a program needn't handle non-finite values.
Results may differ from a plain program's by a relative error of at most 0.0003.
Values sent between devices are 32-bit elements; how exact they have to be, the bound alone decides.
A program may use at most 64 MiB of HBM per device.

v0:
```python
import jax
import jax.numpy as jnp
from jax import lax
from jax.sharding import PartitionSpec as P

epsilon = 1e-05


def transition(rows_block, ln_gain, ln_bias, w_in, w_out):
    average = jnp.mean(rows_block, axis=-1, keepdims=True)
    centred = rows_block - average
    variance = jnp.mean(centred * centred, axis=-1, keepdims=True)
    normed = centred * lax.rsqrt(variance + epsilon) * ln_gain + ln_bias
    projected_in = lax.dot_general(
        normed,
        w_in,
        (((1,), (1,)), ((), ())),
        precision=lax.Precision.HIGHEST,
        preferred_element_type=jnp.float32,
    )
    hidden_units = w_out.shape[0]
    hidden = jax.nn.silu(projected_in[:, :hidden_units]) * projected_in[:, hidden_units:]
    return rows_block + jnp.dot(
        hidden, w_out, precision=lax.Precision.HIGHEST, preferred_element_type=jnp.float32
    )


def group_rows(tile_rows, tile_cols):
    stride_rows = 1
    while (
        stride_rows < tile_rows
        and stride_rows * tile_cols < 1024
        and (tile_rows % (stride_rows * 2) == 0)
    ):
        stride_rows = stride_rows * 2
    return stride_rows


def mirror(tile):
    row_devices = lax.axis_size("row")
    col_devices = lax.axis_size("col")
    factor = col_devices // row_devices
    tile_cols = tile.shape[1]
    channels = tile.shape[2]
    slab_rows = tile_cols // row_devices
    pieces = tile.reshape(factor, row_devices, slab_rows, tile_cols * channels)
    pieces = lax.all_to_all(
        lax.all_to_all(pieces, "row", split_axis=1, concat_axis=0, tiled=True),
        "col",
        split_axis=0,
        concat_axis=0,
        tiled=True,
    )
    pieces = pieces.reshape(row_devices, factor, slab_rows, tile_cols * channels)
    pieces = lax.all_to_all(pieces, "row", split_axis=0, concat_axis=2, tiled=True)
    pieces = pieces.reshape(factor, tile_cols, tile_cols, channels)
    return jnp.transpose(pieces, (0, 2, 1, 3)).reshape(factor * tile_cols, tile_cols, channels)


def on_device(pair_rep, ln_gain, ln_bias, w_in, w_out, w_pde, labels, pair_mask):
    tile_rows, tile_cols, channels = pair_rep.shape
    stride_rows = group_rows(tile_rows, tile_cols)
    blocks = pair_rep.reshape(tile_rows // stride_rows, stride_rows * tile_cols, channels)

    def forward(rows_block):
        return transition(rows_block, ln_gain, ln_bias, w_in, w_out)

    updated = lax.map(forward, blocks).reshape(tile_rows, tile_cols, channels)
    mask_float = pair_mask.astype(jnp.float32)
    local_count = jnp.sum(mask_float)
    valid_count = lax.psum(local_count, ("row", "col"))
    inverse_count = 1.0 / valid_count
    projected = jnp.einsum("ijc,cb->ijb", updated, w_pde, precision=lax.Precision.HIGHEST)
    scores = projected + mirror(projected)
    highest = jnp.max(scores, axis=-1, keepdims=True)
    shifted = jnp.exp(scores - highest)
    exp_total = jnp.sum(shifted, axis=-1, keepdims=True)
    log_total = highest + jnp.log(exp_total)
    bin_index = lax.broadcasted_iota(jnp.int32, (1, 1, scores.shape[2]), 2)
    onehot = (labels[:, :, None] == bin_index).astype(jnp.float32)
    picked = jnp.sum(scores * onehot, axis=-1, keepdims=True)
    local_loss = jnp.sum(mask_float * (log_total - picked)[:, :, 0])
    d_scores = mask_float[:, :, None] * (shifted / exp_total - onehot) * inverse_count
    d_sym = d_scores + mirror(d_scores)
    d_updated = jnp.einsum("ijb,cb->ijc", d_sym, w_pde, precision=lax.Precision.HIGHEST)
    grad_pde = jnp.einsum("ijc,ijb->cb", updated, d_sym, precision=lax.Precision.HIGHEST)
    cot_blocks = d_updated.reshape(blocks.shape)

    def backward(totals, pieces):
        rows_block, cotangent = pieces
        outcome, pullback = jax.vjp(transition, rows_block, ln_gain, ln_bias, w_in, w_out)
        gradients = pullback(cotangent)
        merged = tuple((earlier + later for earlier, later in zip(totals, gradients[1:])))
        return (merged, gradients[0])

    start_sums = (
        jnp.zeros_like(ln_gain),
        jnp.zeros_like(ln_bias),
        jnp.zeros_like(w_in),
        jnp.zeros_like(w_out),
    )
    param_sums, d_blocks = lax.scan(backward, start_sums, (blocks, cot_blocks))
    g_gain, g_bias, g_in, g_out = param_sums
    row_in, row_out = (
        lax.psum_scatter(g_in, "row", scatter_dimension=0, tiled=True),
        lax.psum_scatter(g_out, "row", scatter_dimension=0, tiled=True),
    )
    shard_in, shard_out = (
        lax.psum_scatter(row_in, "col", scatter_dimension=0, tiled=True),
        lax.psum_scatter(row_out, "col", scatter_dimension=0, tiled=True),
    )
    loss_sum, gain_sum, bias_sum, pde_sum = lax.psum(
        (local_loss, g_gain, g_bias, grad_pde), ("row", "col")
    )
    late_scale = 1.0
    mean_loss = loss_sum / valid_count
    d_pair_rep = d_blocks.reshape(pair_rep.shape) * late_scale
    return (
        mean_loss,
        d_pair_rep,
        gain_sum * late_scale,
        bias_sum * late_scale,
        shard_in * late_scale,
        shard_out * late_scale,
        pde_sum * late_scale,
    )


def solution(mesh):
    placed = (P("row", "col", None), P(), P(), P(), P(), P(), P("row", "col"), P("row", "col"))
    return jax.shard_map(
        on_device,
        mesh=mesh,
        in_specs=placed,
        out_specs=(
            P(),
            P("row", "col", None),
            P(),
            P(),
            P(("row", "col"), None),
            P(("row", "col"), None),
            P(),
        ),
        check_vma=False,
    )
```

profile of v0, /device:TPU:0, one launch (start us, length us, event | category | flops | bytes accessed | tf_op | source)
XLA Modules:
  0.0 227.3 jit_solution(3535305278162302303)
XLA Ops:
  7.2 0.0 copy-start
  7.2 0.0 copy-start.1
  7.2 1.0 reduce_sum.109
  8.2 0.1 div.52
  8.3 0.0 copy-done.1
  8.3 0.2 multiply_reduce_fusion.2
  8.5 0.1 add.95
  8.6 0.0 copy-start.3
  8.6 0.0 copy-start.6
  8.6 0.0 copy-done
  8.6 0.6 copy-done.3
  9.2 0.0 copy-done.6
  9.2 0.0 copy-start.7
  9.2 0.6 fusion.8
  9.9 0.3 copy-done.7
  10.2 0.0 copy-start.2
  10.2 0.4 fusion
  10.6 0.3 copy-done.2
  11.0 0.2 fusion.10
  11.2 0.1 reshape.118
  11.3 9.7 %all_to_all.76 = f32[2,4,2,512]{3,2,0,1:T(2,128)S(1)} all-to-all(f32[2,4,2,512]{3,2,0,1:T(2,128)S(1)} %copy.34), channel_id=1, replica_groups=mesh['row'=4,'col'=8] {'row'}, dimensions={1} | all-to-all | bytes 65536 | tf_op jit(solution)/shard_map/all_to_all | solution.py:48
  21.0 10.5 %all_to_all.77 = f32[8,1,2,512]{3,2,1,0:T(2,128)} all-to-all(f32[8,1,2,512]{3,2,1,0:T(2,128)S(1)} %bitcast.70), channel_id=1, replica_groups=mesh['row'=4,'col'=8] {'col'}, dimensions={0} | all-to-all | bytes 65536 | tf_op jit(solution)/shard_map/all_to_all | solution.py:47
  31.5 0.0 copy-start.4
  31.5 3.4 %all-to-all-start.2 = ((f32[4,2,2,512]{3,2,1,0:T(2,128)}), f32[4,2,2,512]{3,2,1,0:T(2,128)S(1)}, u32[]{:S(2)}, u32[]{:S(2)}) async-start(f32[4,2,2,512]{3,2,1,0:T(2,128)} %bitcast.7), calls=%async_computation.2 | async-start | bytes 65536 | tf_op jit(solution)/shard_map/all_to_all | solution.py:55
  34.9 0.0 copy-start.5
  34.9 0.0 reduce-scatter.9.cloned.1.call-start
  35.0 0.0 copy-done.4
  35.0 0.1 copy.38
  35.1 0.5 copy-done.5
  35.6 0.1 copy.33
  35.7 4.0 %all-to-all-done.2 = f32[4,2,2,512]{3,2,1,0:T(2,128)S(1)} async-done(((f32[4,2,2,512]{3,2,1,0:T(2,128)}), f32[4,2,2,512]{3,2,1,0:T(2,128)S(1)}, u32[]{:S(2)}, u32[]{:S(2)}) %all-to-all-start.2) | async-done | bytes 32800 | tf_op jit(solution)/shard_map/all_to_all | solution.py:55
  39.7 0.1 reshape.120
  39.8 0.1 fusion.26
  39.9 0.2 fusion.7
  40.1 0.6 convert_reduce_fusion
  40.7 38.5 %psum.36 = f32[]{:T(128)} all-reduce(f32[]{:T(128)} %get-tuple-element.57), channel_id=1, replica_groups=mesh['row'=4,'col'=8] {'row','col'}, use_global_device_ids=true, to_apply=%region_8.9 | all-reduce | flops 1 | bytes 8 | tf_op jit(solution)/shard_map/psum | solution.py:71
  79.9 0.1 multiply_multiply_fusion
  80.0 0.1 reshape.122
  80.1 8.4 %all_to_all.78 = f32[2,4,2,512]{3,2,0,1:T(2,128)S(1)} all-to-all(f32[2,4,2,512]{3,2,0,1:T(2,128)S(1)} %copy.39), channel_id=1, replica_groups=mesh['row'=4,'col'=8] {'row'}, dimensions={1} | all-to-all | bytes 65536 | tf_op jit(solution)/shard_map/all_to_all | solution.py:48
  88.5 8.4 %all_to_all.79 = f32[8,1,2,512]{3,2,1,0:T(2,128)S(1)} all-to-all(f32[8,1,2,512]{3,2,1,0:T(2,128)S(1)} %bitcast.71), channel_id=1, replica_groups=mesh['row'=4,'col'=8] {'col'}, dimensions={0} | all-to-all | bytes 65536 | tf_op jit(solution)/shard_map/all_to_all | solution.py:47
  96.9 7.1 %all_to_all.80 = f32[4,2,2,512]{3,2,1,0:T(2,128)S(1)} all-to-all(f32[4,2,2,512]{3,2,1,0:T(2,128)S(1)} %bitcast.72), channel_id=1, replica_groups=mesh['row'=4,'col'=8] {'row'}, dimensions={0} | all-to-all | bytes 65536 | tf_op jit(solution)/shard_map/all_to_all | solution.py:55
  104.0 0.1 reshape.124
  104.1 0.1 bitcast_add_fusion
  104.3 0.2 convolution_bitcast_fusion
  104.5 1.3 fusion.6
  105.8 0.0 reduce-scatter.9.cloned.1.call-update
  105.8 0.0 reduce-scatter.5.cloned.1.call-start
  105.9 0.4 fusion.23
  106.3 1.8 fusion.1
  108.1 0.0 reduce-scatter.5.cloned.1.call-update
  108.2 0.0 reduce-scatter.11.cloned.1.call-start
  108.2 0.7 multiply_reduce_fusion
  108.9 0.2 fusion.25
  109.2 17.6 %reduce-scatter.9.cloned.1.call-done = f32[128,128]{1,0:T(8,128)} async-done(((f32[512,128]{1,0:T(8,128)}), f32[128,128]{1,0:T(8,128)}) %reduce-scatter.9.cloned.1.call-update) | async-done | bytes 65552 | tf_op jit(solution)/shard_map/reduce_scatter | solution.py:106
  126.8 0.0 reduce-scatter.11.cloned.1.call-update
  126.8 0.0 reduce-scatter.7.cloned.1.call-start
  126.9 27.9 %reduce-scatter.5.cloned.1.call-done = f32[256,128]{1,0:T(8,128)} async-done(((f32[1024,128]{1,0:T(8,128)}), f32[256,128]{1,0:T(8,128)}) %reduce-scatter.5.cloned.1.call-update) | async-done | bytes 131088 | tf_op jit(solution)/shard_map/reduce_scatter | solution.py:105
  154.8 0.0 reduce-scatter.7.cloned.1.call-update
  154.8 0.3 convolution_bitcast_fusion.1
  155.1 40.2 %all-reduce.2 = (f32[]{:T(128)}, f32[128]{0:T(128)}, f32[128]{0:T(128)}, f32[128,64]{0,1:T(8,128)}) all-reduce(f32[]{:T(128)} %get-tuple-element.58, f32[128]{0:T(128)S(1)} %get-tuple-element.52, f32[128]{0:T(128)S(1)} %get-tuple-element.54, f32[128,64]{0,1:T(8,128)S(1)} %convolution_bitcast_fusion.1), channel_id=1, replica_groups=mesh['row'=4,'col'=8] {'row','col'}, use_global_device_ids=true, to_apply=%region_6.7 | all-reduce | flops 8449 | bytes 67592 | tf_op jit(solution)/shard_map/psum | solution.py:112
  196.6 0.7 add_bitcast_fusion
  197.4 0.0 reduce-scatter.11.cloned.1.call-done
  197.4 22.2 %reduce-scatter.7.cloned.1.call-done = f32[32,128]{1,0:T(8,128)} async-done(((f32[256,128]{1,0:T(8,128)}), f32[32,128]{1,0:T(8,128)}) %reduce-scatter.7.cloned.1.call-update) | async-done | bytes 16400 | tf_op jit(solution)/shard_map/reduce_scatter | solution.py:109
  (12 shorter events, 0.1 us)
Async XLA Ops:
  7.2 1.4 copy-start
  7.2 1.1 copy-start.1
  8.6 0.7 copy-start.3
  8.6 0.7 copy-start.6
  9.2 0.9 copy-start.7
  10.2 0.8 copy-start.2
  31.5 3.5 %copy-start.4 = (s32[16,8]{0,1:T(8,128)S(1)}, s32[16,8]{0,1:T(8,128)}, u32[]{:S(2)}) copy-start(s32[16,8]{0,1:T(8,128)} %param.14) | copy-start | bytes 1540
  31.5 8.1 %all-to-all-start.2 = ((f32[4,2,2,512]{3,2,1,0:T(2,128)}), f32[4,2,2,512]{3,2,1,0:T(2,128)S(1)}, u32[]{:S(2)}, u32[]{:S(2)}) async-start(f32[4,2,2,512]{3,2,1,0:T(2,128)} %bitcast.7), calls=%async_computation.2 | async-start | bytes 65536 | tf_op jit(solution)/shard_map/all_to_all | solution.py:55
  34.9 0.7 copy-start.5
  34.9 91.8 %reduce-scatter.9.cloned.1.call-start = ((), (), s32[]{:S(2)}) async-start(), calls=%async_computation.12 | async-start | bytes 327680 | tf_op jit(solution)/shard_map/reduce_scatter | solution.py:106
  105.8 49.0 %reduce-scatter.5.cloned.1.call-start = ((), (), s32[]{:S(2)}) async-start(), calls=%async_computation.10 | async-start | bytes 655360 | tf_op jit(solution)/shard_map/reduce_scatter | solution.py:105
  108.2 89.2 %reduce-scatter.11.cloned.1.call-start = ((), (), s32[]{:S(2)}) async-start(), calls=%async_computation.13 | async-start | bytes 73728 | tf_op jit(solution)/shard_map/reduce_scatter | solution.py:110
  126.8 92.8 %reduce-scatter.7.cloned.1.call-start = ((), (), s32[]{:S(2)}) async-start(), calls=%async_computation.11 | async-start | bytes 147456 | tf_op jit(solution)/shard_map/reduce_scatter | solution.py:109
Sparse Core Ops, SparseCore 0:
  105.9 20.8 reduce-scatter.8
  129.6 25.1 reduce-scatter.4
  157.6 30.5 reduce-scatter.10
  190.8 28.7 reduce-scatter.6
where the time goes:
time: 228 us; the launch traced here: 227 us
  blocking collectives  123 us (54%)
  waiting for transfers between devices  71.8 us (31%)
  between operations  17.2 us (8%)
  matrix products  6.04 us (3%)
  starting transfers between devices  3.56 us (2%)
  other arithmetic  3.27 us (1%)
  local copies, waits for them, and re-layouts  2.58 us (1%)
    psum x1, blocking collectives, on_device(): lax.psum((local_loss, g_gain, g_bias, grad_pde), ('row', 'col'))  40.2 us
    psum x1, blocking collectives, on_device(): valid_count = lax.psum(local_count, ('row', 'col'))  38.5 us
    reduce_scatter x1, waiting for transfers between devices, on_device(): lax.psum_scatter(g_in, 'row', scatter_dimension=0, tiled=True)  27.9 us
    reduce_scatter x1, waiting for transfers between devices, on_device(): lax.psum_scatter(row_in, 'col', scatter_dimension=0, tiled=True)  22.2 us
    all_to_all x2, blocking collectives, mirror(): lax.all_to_all(lax.all_to_all(pieces, 'row', split_axis=1, concat_axis=0,...  18.9 us
    all_to_all x2, blocking collectives, mirror(): lax.all_to_all(pieces, 'row', split_axis=1, concat_axis=0, tiled=True)  18.1 us
    reduce_scatter x1, waiting for transfers between devices, on_device(): lax.psum_scatter(g_out, 'row', scatter_dimension=0, tiled=True)  17.6 us
    all_to_all x1, blocking collectives, mirror(): lax.all_to_all(pieces, 'row', split_axis=0, concat_axis=2, tiled=True)  7.1 us
  transfers between devices with their start and end apart: 5, of which 4 were waited for; matrix products, arithmetic and copies ran while one was open for 2% of the time, Pallas kernels for 0%

commit v1 on v0

--- a/solution.py
+++ b/solution.py
@@ -4,6 +4,28 @@
 from jax.sharding import PartitionSpec as P
 
 epsilon = 1e-05
+
+
+def in_blocks(shard, dim, count):
+    before, after = (shard.shape[:dim], shard.shape[dim + 1 :])
+    return jnp.moveaxis(shard.reshape(*before, count, -1, *after), dim, 0)
+
+
+def joined_along(blocks, dim):
+    shape = list(blocks.shape[1:])
+    shape[dim] *= blocks.shape[0]
+    return jnp.moveaxis(blocks, 0, dim).reshape(shape)
+
+
+def rotated_exchange(x, axis, split_dim, concat_dim):
+    size, index = (lax.axis_size(axis), lax.axis_index(axis))
+    blocks = in_blocks(x, split_dim, size)
+    outs = [blocks[index]]
+    for step in range(1, size):
+        sent = blocks[(index + step) % size]
+        outs.append(lax.ppermute(sent, axis, [(i, (i + step) % size) for i in range(size)]))
+    blocks = jnp.stack(outs)[(index - jnp.arange(size)) % size]
+    return joined_along(blocks, concat_dim)
 
 
 def transition(rows_block, ln_gain, ln_bias, w_in, w_out):
@@ -45,11 +67,7 @@
     slab_rows = tile_cols // row_devices
     pieces = tile.reshape(factor, row_devices, slab_rows, tile_cols * channels)
     pieces = lax.all_to_all(
-        lax.all_to_all(pieces, "row", split_axis=1, concat_axis=0, tiled=True),
-        "col",
-        split_axis=0,
-        concat_axis=0,
-        tiled=True,
+        rotated_exchange(pieces, "row", 1, 0), "col", split_axis=0, concat_axis=0, tiled=True
     )
     pieces = pieces.reshape(row_devices, factor, slab_rows, tile_cols * channels)
     pieces = lax.all_to_all(pieces, "row", split_axis=0, concat_axis=2, tiled=True)

time: 228 us -> 229 us (level)
  blocking collectives: 123 us -> 105 us
  starting transfers between devices: 3.56 us -> 13.2 us
  waiting for transfers between devices: 71.8 us -> 79.5 us
    all_to_all x4 -> x2, blocking collectives: 37 us -> 18.9 us  [mirror(): lax.all_to_all(rotated_exchange(pieces, 'row', 1, 0), 'col', split_axis=0...]
    ppermute x0 -> x6, starting transfers between devices: none -> 9.62 us  [rotated_exchange(): lax.ppermute(sent, axis, [(i, (i + step) % size) for i in range(size)])]
    ppermute x0 -> x6, waiting for transfers between devices: none -> 7.72 us  [rotated_exchange(): lax.ppermute(sent, axis, [(i, (i + step) % size) for i in range(size)])]
  transfers between devices with their start and end apart: 5 -> 11, of which waited for: 4 -> 9; matrix products, arithmetic and copies ran while one was open for 2% -> 2% of each run, Pallas kernels for 0% -> 0%
where the time goes in v1:
time: 229 us; the launch traced here: 228 us
  blocking collectives  105 us (46%)
  waiting for transfers between devices  79.5 us (35%)
  between operations  17.2 us (8%)
  starting transfers between devices  13.2 us (6%)
  matrix products  6.04 us (3%)
  local copies, waits for them, and re-layouts  4.63 us (2%)
  other arithmetic  2.42 us (1%)
    psum x1, blocking collectives, on_device(): lax.psum((local_loss, g_gain, g_bias, grad_pde), ('row', 'col'))  40.2 us
    psum x1, blocking collectives, on_device(): valid_count = lax.psum(local_count, ('row', 'col'))  38.5 us
    reduce_scatter x1, waiting for transfers between devices, on_device(): lax.psum_scatter(g_in, 'row', scatter_dimension=0, tiled=True)  27.9 us
    reduce_scatter x1, waiting for transfers between devices, on_device(): lax.psum_scatter(row_in, 'col', scatter_dimension=0, tiled=True)  22.2 us
    all_to_all x2, blocking collectives, mirror(): lax.all_to_all(rotated_exchange(pieces, 'row', 1, 0), 'col', split_axis=0...  18.9 us
    reduce_scatter x1, waiting for transfers between devices, on_device(): lax.psum_scatter(g_out, 'row', scatter_dimension=0, tiled=True)  17.6 us
    ppermute x6, starting transfers between devices, rotated_exchange(): lax.ppermute(sent, axis, [(i, (i + step) % size) for i in range(size)])  9.62 us
    ppermute x6, waiting for transfers between devices, rotated_exchange(): lax.ppermute(sent, axis, [(i, (i + step) % size) for i in range(size)])  7.72 us
  transfers between devices with their start and end apart: 11, of which 9 were waited for; matrix products, arithmetic and copies ran while one was open for 2% of the time, Pallas kernels for 0%

profile of v1, /device:TPU:0, one launch (start us, length us, event | category | flops | bytes accessed | tf_op | source)
XLA Modules:
  0.0 227.7 jit_solution(12321743313024409734)
XLA Ops:
  7.2 0.0 copy-start
  7.2 0.8 copy-done.1
  8.1 0.1 reduce_sum.109
  8.2 0.1 div.52
  8.3 0.2 multiply_reduce_fusion.2
  8.4 0.1 add.162
  8.6 0.6 copy-done.3
  9.2 0.0 copy-done.6
  9.2 0.6 fusion.8
  9.8 0.3 copy-done.7
  10.2 0.4 fusion
  10.6 0.3 copy-done.2
  10.9 0.2 fusion.10
  11.1 0.1 reshape_reshape.6
  11.3 4.0 %collective-permute-start.2 = (f32[2,1,2,512]{3,2,0,1:T(2,128)S(1)}, f32[2,1,2,512]{3,2,0,1:T(2,128)S(1)}, u32[]{:S(2)}, u32[]{:S(2)}) collective-permute-start(f32[2,1,2,512]{3,2,0,1:T(2,128)S(1)} %get-tuple-element.86), channel_id=1, source_target_pairs={{0,24},{8,0},{16,8},{24,16},{1,25},{9,1},{17,9},{25,17},{2,26},{10... | collective-permute-start | bytes 24584 | tf_op jit(solution)/shard_map/ppermute | solution.py:26
  15.2 0.5 collective-permute-start.1
  15.7 0.6 collective-permute-start
  16.4 0.2 collective-permute-done.2
  16.6 2.3 %collective-permute-done.1 = f32[2,1,2,512]{3,2,0,1:T(2,128)S(1)} collective-permute-done((f32[2,1,2,512]{3,2,0,1:T(2,128)S(1)}, f32[2,1,2,512]{3,2,0,1:T(2,128)S(1)}, u32[]{:S(2)}, u32[]{:S(2)}) %collective-permute-start.1) | collective-permute-done | bytes 8224 | tf_op jit(solution)/shard_map/ppermute | solution.py:26
  18.9 1.4 collective-permute-done
  20.3 0.6 gather_fusion
  20.9 10.5 %all_to_all.40 = f32[8,1,2,512]{3,2,1,0:T(2,128)} all-to-all(f32[8,1,2,512]{3,2,1,0:T(2,128)S(1)} %bitcast.87), channel_id=1, replica_groups=mesh['row'=4,'col'=8] {'col'}, dimensions={0} | all-to-all | bytes 65536 | tf_op jit(solution)/shard_map/all_to_all | solution.py:69
  31.4 3.4 %all-to-all-start.1 = ((f32[4,2,2,512]{3,2,1,0:T(2,128)}), f32[4,2,2,512]{3,2,1,0:T(2,128)S(1)}, u32[]{:S(2)}, u32[]{:S(2)}) async-start(f32[4,2,2,512]{3,2,1,0:T(2,128)} %bitcast.13), calls=%async_computation.1 | async-start | bytes 65536 | tf_op jit(solution)/shard_map/all_to_all | solution.py:73
  34.8 0.0 reduce-scatter.9.cloned.1.call-start
  34.9 0.1 copy.40
  35.0 0.5 copy-done.5
  35.5 0.1 copy.37
  35.6 4.0 %all-to-all-done.1 = f32[4,2,2,512]{3,2,1,0:T(2,128)S(1)} async-done(((f32[4,2,2,512]{3,2,1,0:T(2,128)}), f32[4,2,2,512]{3,2,1,0:T(2,128)S(1)}, u32[]{:S(2)}, u32[]{:S(2)}) %all-to-all-start.1) | async-done | bytes 32800 | tf_op jit(solution)/shard_map/all_to_all | solution.py:73
  39.6 0.1 reshape.183
  39.7 0.1 fusion.28
  39.8 0.2 fusion.7
  40.0 0.6 convert_reduce_fusion
  40.6 38.5 %psum.36 = f32[]{:T(128)} all-reduce(f32[]{:T(128)} %get-tuple-element.57), channel_id=1, replica_groups=mesh['row'=4,'col'=8] {'row','col'}, use_global_device_ids=true, to_apply=%region_8.9 | all-reduce | flops 1 | bytes 8 | tf_op jit(solution)/shard_map/psum | solution.py:89
  79.8 0.1 multiply_multiply_fusion
  79.9 0.1 reshape_reshape.7
  80.0 2.6 %collective-permute-start.5 = (f32[2,1,2,512]{3,2,0,1:T(2,128)S(1)}, f32[2,1,2,512]{3,2,0,1:T(2,128)S(1)}, u32[]{:S(2)}, u32[]{:S(2)}) collective-permute-start(f32[2,1,2,512]{3,2,0,1:T(2,128)S(1)} %get-tuple-element.82), channel_id=1, source_target_pairs={{0,24},{8,0},{16,8},{24,16},{1,25},{9,1},{17,9},{25,17},{2,26},{10... | collective-permute-start | bytes 24584 | tf_op jit(solution)/shard_map/ppermute | solution.py:26
  82.7 1.2 collective-permute-start.4
  83.8 0.8 collective-permute-start.3
  84.6 1.7 collective-permute-done.4
  86.3 2.1 collective-permute-done.3
  88.4 0.6 gather_fusion.1
  89.0 8.4 %all_to_all.41 = f32[8,1,2,512]{3,2,1,0:T(2,128)S(1)} all-to-all(f32[8,1,2,512]{3,2,1,0:T(2,128)S(1)} %bitcast.86), channel_id=1, replica_groups=mesh['row'=4,'col'=8] {'col'}, dimensions={0} | all-to-all | bytes 65536 | tf_op jit(solution)/shard_map/all_to_all | solution.py:69
  97.4 7.1 %all_to_all.42 = f32[4,2,2,512]{3,2,1,0:T(2,128)S(1)} all-to-all(f32[4,2,2,512]{3,2,1,0:T(2,128)S(1)} %bitcast.88), channel_id=1, replica_groups=mesh['row'=4,'col'=8] {'row'}, dimensions={0} | all-to-all | bytes 65536 | tf_op jit(solution)/shard_map/all_to_all | solution.py:73
  104.5 0.1 reshape.187
  104.6 0.1 bitcast_add_fusion
  104.7 0.2 convolution_bitcast_fusion
  104.9 1.3 fusion.6
  106.3 0.0 reduce-scatter.9.cloned.1.call-update
  106.3 0.0 reduce-scatter.5.cloned.1.call-start
  106.3 0.4 fusion.25
  106.8 1.8 fusion.1
  108.6 0.0 reduce-scatter.5.cloned.1.call-update
  108.6 0.0 reduce-scatter.11.cloned.1.call-start
  108.7 0.7 multiply_reduce_fusion
  109.4 0.2 fusion.27
  109.6 17.6 %reduce-scatter.9.cloned.1.call-done = f32[128,128]{1,0:T(8,128)} async-done(((f32[512,128]{1,0:T(8,128)}), f32[128,128]{1,0:T(8,128)}) %reduce-scatter.9.cloned.1.call-update) | async-done | bytes 65552 | tf_op jit(solution)/shard_map/reduce_scatter | solution.py:124
  127.3 0.0 reduce-scatter.11.cloned.1.call-update
  127.3 0.0 reduce-scatter.7.cloned.1.call-start
  127.3 27.9 %reduce-scatter.5.cloned.1.call-done = f32[256,128]{1,0:T(8,128)} async-done(((f32[1024,128]{1,0:T(8,128)}), f32[256,128]{1,0:T(8,128)}) %reduce-scatter.5.cloned.1.call-update) | async-done | bytes 131088 | tf_op jit(solution)/shard_map/reduce_scatter | solution.py:123
  155.2 0.0 reduce-scatter.7.cloned.1.call-update
  155.3 0.3 convolution_bitcast_fusion.1
  155.5 40.2 %all-reduce.2 = (f32[]{:T(128)}, f32[128]{0:T(128)}, f32[128]{0:T(128)}, f32[128,64]{0,1:T(8,128)}) all-reduce(f32[]{:T(128)} %get-tuple-element.58, f32[128]{0:T(128)S(1)} %get-tuple-element.52, f32[128]{0:T(128)S(1)} %get-tuple-element.54, f32[128,64]{0,1:T(8,128)S(1)} %convolution_bitcast_fusion.1), channel_id=1, replica_groups=mesh['row'=4,'col'=8] {'row','col'}, use_global_device_ids=true, to_apply=%region_6.7 | all-reduce | flops 8449 | bytes 67592 | tf_op jit(solution)/shard_map/psum | solution.py:130
  197.1 0.7 add_bitcast_fusion
  197.8 22.2 %reduce-scatter.7.cloned.1.call-done = f32[32,128]{1,0:T(8,128)} async-done(((f32[256,128]{1,0:T(8,128)}), f32[32,128]{1,0:T(8,128)}) %reduce-scatter.7.cloned.1.call-update) | async-done | bytes 16400 | tf_op jit(solution)/shard_map/reduce_scatter | solution.py:127
  (27 shorter events, 0.2 us)
Async XLA Ops:
  7.2 1.4 copy-start
  7.2 0.9 copy-start.1
  8.5 0.7 copy-start.3
  8.5 0.7 copy-start.6
  9.2 0.9 copy-start.7
  10.2 0.8 copy-start.2
  11.3 5.3 %collective-permute-start.2 = (f32[2,1,2,512]{3,2,0,1:T(2,128)S(1)}, f32[2,1,2,512]{3,2,0,1:T(2,128)S(1)}, u32[]{:S(2)}, u32[]{:S(2)}) collective-permute-start(f32[2,1,2,512]{3,2,0,1:T(2,128)S(1)} %get-tuple-element.86), channel_id=1, source_target_pairs={{0,24},{8,0},{16,8},{24,16},{1,25},{9,1},{17,9},{25,17},{2,26},{10... | collective-permute-start | bytes 24584 | tf_op jit(solution)/shard_map/ppermute | solution.py:26
  15.2 3.7 %collective-permute-start.1 = (f32[2,1,2,512]{3,2,0,1:T(2,128)S(1)}, f32[2,1,2,512]{3,2,0,1:T(2,128)S(1)}, u32[]{:S(2)}, u32[]{:S(2)}) collective-permute-start(f32[2,1,2,512]{3,2,0,1:T(2,128)S(1)} %get-tuple-element.87), channel_id=1, source_target_pairs={{0,16},{8,24},{16,0},{24,8},{1,17},{9,25},{17,1},{25,9},{2,18},{10... | collective-permute-start | bytes 24584 | tf_op jit(solution)/shard_map/ppermute | solution.py:26
  15.7 4.5 %collective-permute-start = (f32[2,1,2,512]{3,2,0,1:T(2,128)S(1)}, f32[2,1,2,512]{3,2,0,1:T(2,128)S(1)}, u32[]{:S(2)}, u32[]{:S(2)}) collective-permute-start(f32[2,1,2,512]{3,2,0,1:T(2,128)S(1)} %get-tuple-element.88), channel_id=1, source_target_pairs={{0,8},{8,16},{16,24},{24,0},{1,9},{9,17},{17,25},{25,1},{2,10},{10... | collective-permute-start | bytes 24584 | tf_op jit(solution)/shard_map/ppermute | solution.py:26
  31.4 3.5 %copy-start.4 = (s32[16,8]{0,1:T(8,128)S(1)}, s32[16,8]{0,1:T(8,128)}, u32[]{:S(2)}) copy-start(s32[16,8]{0,1:T(8,128)} %param.14) | copy-start | bytes 1540
  31.4 8.1 %all-to-all-start.1 = ((f32[4,2,2,512]{3,2,1,0:T(2,128)}), f32[4,2,2,512]{3,2,1,0:T(2,128)S(1)}, u32[]{:S(2)}, u32[]{:S(2)}) async-start(f32[4,2,2,512]{3,2,1,0:T(2,128)} %bitcast.13), calls=%async_computation.1 | async-start | bytes 65536 | tf_op jit(solution)/shard_map/all_to_all | solution.py:73
  34.8 0.7 copy-start.5
  34.8 92.4 %reduce-scatter.9.cloned.1.call-start = ((), (), s32[]{:S(2)}) async-start(), calls=%async_computation.10 | async-start | bytes 327680 | tf_op jit(solution)/shard_map/reduce_scatter | solution.py:124
  80.0 4.5 %collective-permute-start.5 = (f32[2,1,2,512]{3,2,0,1:T(2,128)S(1)}, f32[2,1,2,512]{3,2,0,1:T(2,128)S(1)}, u32[]{:S(2)}, u32[]{:S(2)}) collective-permute-start(f32[2,1,2,512]{3,2,0,1:T(2,128)S(1)} %get-tuple-element.82), channel_id=1, source_target_pairs={{0,24},{8,0},{16,8},{24,16},{1,25},{9,1},{17,9},{25,17},{2,26},{10... | collective-permute-start | bytes 24584 | tf_op jit(solution)/shard_map/ppermute | solution.py:26
  82.7 3.7 %collective-permute-start.4 = (f32[2,1,2,512]{3,2,0,1:T(2,128)S(1)}, f32[2,1,2,512]{3,2,0,1:T(2,128)S(1)}, u32[]{:S(2)}, u32[]{:S(2)}) collective-permute-start(f32[2,1,2,512]{3,2,0,1:T(2,128)S(1)} %get-tuple-element.83), channel_id=1, source_target_pairs={{0,16},{8,24},{16,0},{24,8},{1,17},{9,25},{17,1},{25,9},{2,18},{10... | collective-permute-start | bytes 24584 | tf_op jit(solution)/shard_map/ppermute | solution.py:26
  83.8 4.5 %collective-permute-start.3 = (f32[2,1,2,512]{3,2,0,1:T(2,128)S(1)}, f32[2,1,2,512]{3,2,0,1:T(2,128)S(1)}, u32[]{:S(2)}, u32[]{:S(2)}) collective-permute-start(f32[2,1,2,512]{3,2,0,1:T(2,128)S(1)} %get-tuple-element.84), channel_id=1, source_target_pairs={{0,8},{8,16},{16,24},{24,0},{1,9},{9,17},{17,25},{25,1},{2,10},{10... | collective-permute-start | bytes 24584 | tf_op jit(solution)/shard_map/ppermute | solution.py:26
  106.3 49.0 %reduce-scatter.5.cloned.1.call-start = ((), (), s32[]{:S(2)}) async-start(), calls=%async_computation.8 | async-start | bytes 655360 | tf_op jit(solution)/shard_map/reduce_scatter | solution.py:123
  108.6 89.2 %reduce-scatter.11.cloned.1.call-start = ((), (), s32[]{:S(2)}) async-start(), calls=%async_computation.11 | async-start | bytes 73728 | tf_op jit(solution)/shard_map/reduce_scatter | solution.py:128
  127.3 92.8 %reduce-scatter.7.cloned.1.call-start = ((), (), s32[]{:S(2)}) async-start(), calls=%async_computation.9 | async-start | bytes 147456 | tf_op jit(solution)/shard_map/reduce_scatter | solution.py:127
Sparse Core Ops, SparseCore 0:
  106.4 20.8 reduce-scatter.8
  130.1 25.1 reduce-scatter.4
  158.1 30.5 reduce-scatter.10
  191.3 28.7 reduce-scatter.6
